TPU v7x, 32 devices: a whole 2x2x4 slice. The times are simulated.
32 devices in a mesh: groups: 2 (over y), tile: 4 (over z), pair: 2 (over x), sub: 2 (over core).
Axes of the slice: x: 2, y: 2, z: 4, core: 2. Of those that a mesh axis runs over, the one named last changes fastest.
Arguments:
- ref_chips: bfloat16 [4, 256, 4096], P(('groups', 'pair'), ('tile', 'sub')), parts along dimension 0, may hold values from -300 to 700
- search_windows: bfloat16 [4, 512, 16384], P(('groups', 'pair'), ('tile', 'sub')), parts along dimension 0, may hold values from -300 to 700
- dest_block: int32 [4, 512, 1], P(('groups', 'pair'), ('tile', 'sub')), parts along dimension 0, may hold values from 0 to 7; in each aligned block of 64 rows (0 to 63, 64 to 127, ..., all dimensions but the last counted through in order) at most 16 rows name the same one
- dest_slot: int32 [4, 512], P(('groups', 'pair'), ('tile', 'sub')), parts along dimension 0, may hold values from 0 to 31
Outputs:
- smoothed_scores: float32 [4, 256, 4096], P(('groups', 'pair'), ('tile', 'sub')), parts along dimension 0
There are 2 independent parts, one for each index of `groups`. A program takes and returns all parts, laid end to end along the dimension named above; each array names one. Nothing has to cross between parts.
Inputs may be any that keep to these rules, and one draw needn't show every extreme that they name: `dest_block`: in the rows of one device (aligned blocks of 64 windows), no block index is named by more than 16 windows.
All inputs are finite; a program needn't handle non-finite values.
Results may differ from a plain program's by a relative error of at most 0.0003.
Values may be sent and summed in bfloat16 or wider, within the bound.
No kernel may reach another device: no remote copies, remote signals or barrier semaphores. Data moves between devices by JAX's collectives and lax.ppermute only.
A program may use at most 64 MiB of HBM per device.

v0:
```python
import math
import jax
import jax.numpy as jnp
from jax import lax
from jax.sharding import PartitionSpec as P

CHIP = 64
WIN = 128
GC = 8
precise = lax.Precision.HIGHEST
epsilon = 1e-06


def padded(block, sides, width):
    for axis, dim in sides:
        count = lax.axis_size(axis)
        forward = [(i, i + 1) for i in range(count - 1)]
        backward = [(target, source) for source, target in forward]
        low = lax.ppermute(
            lax.slice_in_dim(block, block.shape[dim] - width, None, axis=dim), axis, forward
        )
        high = lax.ppermute(lax.slice_in_dim(block, 0, width, axis=dim), axis, backward)
        block = jnp.concatenate([low, block, high], axis=dim)
    return block


def tables(length, width):
    freqs = jnp.arange(length, dtype=jnp.int32)[:, None]
    places = jnp.arange(width, dtype=jnp.int32)[None, :]
    phase = freqs * places % length
    angle = phase.astype(jnp.float32) * (2.0 * math.pi / length)
    return (jnp.cos(angle), jnp.sin(angle))


def spectrum(image, cosine, sine_table):
    first_real = jnp.einsum("kn,bnm->bkm", cosine, image, precision=precise)
    first_imag = -jnp.einsum("kn,bnm->bkm", sine_table, image, precision=precise)
    spec_real = jnp.einsum("bkm,lm->bkl", first_real, cosine, precision=precise) + jnp.einsum(
        "bkm,lm->bkl", first_imag, sine_table, precision=precise
    )
    spec_imag = jnp.einsum("bkm,lm->bkl", first_imag, cosine, precision=precise) - jnp.einsum(
        "bkm,lm->bkl", first_real, sine_table, precision=precise
    )
    return (spec_real, spec_imag)


def centre(chips_raw, chip_side):
    chip_float = chips_raw.astype(jnp.float32).reshape(-1, chip_side, chip_side)
    centred = chip_float - jnp.mean(chip_float, axis=(1, 2), keepdims=True)
    chip_std = jnp.sqrt(jnp.mean(centred * centred, axis=(1, 2)) + epsilon)
    return (centred, chip_std)


def match(chip_real, chip_imag, chip_std, windows_raw, chip_side, window_side):
    offsets = window_side - chip_side
    cos_full, sin_full = tables(window_side, window_side)
    cos_part = cos_full[:offsets]
    sin_part = sin_full[:offsets]
    window_float = windows_raw.astype(jnp.float32).reshape(-1, window_side, window_side)
    win_real, win_imag = spectrum(window_float, cos_full, sin_full)
    product_real = chip_real * win_real + chip_imag * win_imag
    product_imag = chip_real * win_imag - chip_imag * win_real
    half_real = jnp.einsum("ak,bkl->bal", cos_part, product_real, precision=precise) - jnp.einsum(
        "ak,bkl->bal", sin_part, product_imag, precision=precise
    )
    half_imag = jnp.einsum("ak,bkl->bal", cos_part, product_imag, precision=precise) + jnp.einsum(
        "ak,bkl->bal", sin_part, product_real, precision=precise
    )
    numerator = (
        jnp.einsum("bal,el->bae", half_real, cos_part, precision=precise)
        - jnp.einsum("bal,el->bae", half_imag, sin_part, precision=precise)
    ) / (window_side * window_side)
    starts = jnp.arange(offsets, dtype=jnp.int32)[:, None]
    pixels = jnp.arange(window_side, dtype=jnp.int32)[None, :]
    window_band = ((pixels >= starts) & (pixels < starts + chip_side)).astype(jnp.float32)
    first_rows = jnp.einsum("ax,bxy->bay", window_band, window_float, precision=precise)
    first_sum = jnp.einsum("bay,ey->bae", first_rows, window_band, precision=precise)
    second_rows = jnp.einsum(
        "ax,bxy->bay", window_band, window_float * window_float, precision=precise
    )
    second_sum = jnp.einsum("bay,ey->bae", second_rows, window_band, precision=precise)
    patch_mean = first_sum / (chip_side * chip_side)
    patch_var = second_sum / (chip_side * chip_side) - patch_mean * patch_mean
    score = numerator / (chip_side * chip_std[:, None, None] * jnp.sqrt(patch_var + epsilon))
    return score.reshape(-1, offsets * offsets)


def in_blocks(function, operands):
    amount = operands[0].shape[0]
    block_rows = 16
    shaped = tuple(
        (item.reshape((amount // block_rows, block_rows) + item.shape[1:]) for item in operands)
    )
    result = lax.map(lambda grouped: function(*grouped), shaped)
    return result.reshape(amount, -1)


def on_device(ref_chips, search_windows, dest_block, dest_slot):
    chips = ref_chips[0]
    windows = search_windows[0]
    targets = dest_block[0, :, 0]
    target_slot = dest_slot[0]
    chip_side = CHIP
    window_side = WIN
    offsets = window_side - chip_side
    window_amount = windows.shape[0]
    chip_amount = chips.shape[0]
    devices = lax.axis_size(("tile", "sub"))
    capacity = max(2, 2 * window_amount // devices)
    slot_amount = devices * capacity
    order = jnp.arange(window_amount, dtype=jnp.int32)
    matches = targets[:, None] == targets[None, :]
    earlier = order[:, None] > order[None, :]
    ranking = jnp.sum((matches & earlier).astype(jnp.int32), axis=1)
    positions = targets * capacity + ranking
    slot_buffer = jnp.full((slot_amount,), -1, jnp.int32).at[positions].set(target_slot)
    cos_chip, sin_chip = tables(window_side, chip_side)
    requests = slot_buffer.reshape(devices, capacity)
    found = jnp.take(
        chips,
        jnp.maximum(
            lax.all_to_all(requests, ("tile", "sub"), split_axis=0, concat_axis=0, tiled=True), 0
        ),
        axis=0,
    )
    fetched = lax.all_to_all(found, ("tile", "sub"), split_axis=0, concat_axis=0, tiled=True)
    own_chips = jnp.take(fetched.reshape(slot_amount, chip_side * chip_side), positions, axis=0)

    def match_own(chip_part, window_part):
        centred_part, std_part = centre(chip_part, chip_side)
        real_part, imag_part = spectrum(centred_part, cos_chip, sin_chip)
        return match(real_part, imag_part, std_part, window_part, chip_side, window_side)

    own_scores = in_blocks(match_own, (own_chips, windows))
    score_buffer = (
        jnp.zeros((slot_amount, offsets * offsets), jnp.float32).at[positions].set(own_scores)
    )
    scores, slots_here = (
        lax.all_to_all(score_buffer, ("tile", "sub"), split_axis=0, concat_axis=0, tiled=True),
        lax.all_to_all(slot_buffer, ("tile", "sub"), split_axis=0, concat_axis=0, tiled=True),
    )
    hits_table = (slots_here[None, :] == jnp.arange(chip_amount, dtype=jnp.int32)[:, None]).astype(
        jnp.float32
    )
    total = jnp.dot(hits_table, scores, precision=precise)
    looks = jnp.sum(hits_table, axis=1)
    average = total / jnp.maximum(looks, 1.0)[:, None]
    grid = average.reshape(-1, GC, offsets * offsets)
    extended = padded(grid, ((("tile", "sub"), 0),), 1)
    vertical = extended[:-2] + extended[2:]
    sideways = jnp.pad(grid, ((0, 0), (1, 1), (0, 0)))
    horizontal = sideways[:, :-2] + sideways[:, 2:]
    smoothed = (4.0 * grid + vertical + horizontal) / 8.0
    return smoothed.reshape(1, chip_amount, offsets * offsets)


def solution(mesh):
    return jax.shard_map(
        on_device,
        mesh=mesh,
        in_specs=(
            P(("groups", "pair"), ("tile", "sub"), None),
            P(("groups", "pair"), ("tile", "sub"), None),
            P(("groups", "pair"), ("tile", "sub"), None),
            P(("groups", "pair"), ("tile", "sub")),
        ),
        out_specs=P(("groups", "pair"), ("tile", "sub"), None),
        check_vma=False,
    )
```

profile of v0, /device:TPU:1, one launch (start us, length us, event | category | flops | bytes accessed | tf_op | source)
XLA Modules:
  0.0 226.2 jit_solution(14719844709658617581)
XLA Ops:
  2.6 11.0 %all_to_all.35 = s32[8,1,16]{2,1,0:T(1,128)S(1)} all-to-all(s32[8,1,16]{2,1,0:T(1,128)S(1)} %bitcast.236), channel_id=1, replica_groups=mesh['groups'=2,'tile'=4,'pair'=2,'sub'=2] {'tile','sub'}, dimensions={0} | all-to-all | bytes 1024 | tf_op jit(solution)/shard_map/all_to_all | solution.py:122
  16.1 4.2 %all-to-all-start.2 = ((bf16[8,16,4096]{2,1,0:T(8,128)(2,1)}), bf16[8,16,4096]{2,1,0:T(8,128)(2,1)S(1)}, u32[]{:S(2)}, u32[]{:S(2)}) async-start(bf16[8,16,4096]{2,1,0:T(8,128)(2,1)} %broadcast_select_fusion), calls=%async_computation.2 | async-start | bytes 2097152 | tf_op jit(solution)/shard_map/all_to_all | solution.py:126
  21.1 24.7 %all-to-all-done.2 = bf16[8,16,4096]{2,1,0:T(8,128)(2,1)S(1)} async-done(((bf16[8,16,4096]{2,1,0:T(8,128)(2,1)}), bf16[8,16,4096]{2,1,0:T(8,128)(2,1)S(1)}, u32[]{:S(2)}, u32[]{:S(2)}) %all-to-all-start.2) | async-done | bytes 1048608 | tf_op jit(solution)/shard_map/all_to_all | solution.py:126
  45.9 4.2 %all-to-all-start = ((s32[8,16,1]{1,2,0:T(1,128)}), s32[8,16,1]{1,2,0:T(1,128)S(1)}, u32[]{:S(2)}, u32[]{:S(2)}) async-start(s32[8,16,1]{1,2,0:T(1,128)} %bitcast.5), calls=%async_computation | async-start | bytes 8192 | tf_op jit(solution)/shard_map/all_to_all | solution.py:140
  51.0 109.2 %while.14 = (s32[]{:T(128)}, f32[4,16,4096]{2,1,0:T(8,128)S(1)}, bf16[4,16,4096]{2,1,0:T(8,128)(2,1)S(1)}, bf16[4,16,16384]{2,1,0:T(8,128)(2,1)}, s32[]{:T(128)}) while((s32[]{:T(128)}, f32[4,16,4096]{2,1,0:T(8,128)S(1)}, bf16[4,16,4096]{2,1,0:T(8,128)(2,1)S(1)}, bf16[4,16,16384]{2,1,0:T(8,128)(2,1)}, s32[]{:T(128)}) %tuple.39), condition=%wide.region_5.6_spmd.clone.clone, body=%wide.region_2.5_spmd.clone.clone.sunk | while | flops 4872994816 | bytes 46598104 | solution.py:94
  58.1 2.0 fusion.248
  60.1 1.9 convolution_add_fusion.5
  62.1 1.9 fusion.252
  64.0 1.9 convolution_subtract_fusion.5
  71.5 1.9 multiply_subtract_fusion.2
  85.4 2.0 fusion.248
  87.4 1.9 convolution_add_fusion.5
  89.3 1.9 fusion.252
  91.3 1.9 convolution_subtract_fusion.5
  98.7 1.9 multiply_subtract_fusion.2
  112.7 2.0 fusion.248
  114.6 1.9 convolution_add_fusion.5
  116.6 1.9 fusion.252
  118.5 1.9 convolution_subtract_fusion.5
  122.3 1.8 convolution_add_fusion.6
  126.0 1.9 multiply_subtract_fusion.2
  139.9 2.0 fusion.248
  141.9 1.9 convolution_add_fusion.5
  143.8 1.9 fusion.252
  145.8 1.9 convolution_subtract_fusion.5
  153.2 1.9 multiply_subtract_fusion.2
  160.3 2.6 %scatter_custom_fusion.1 = f32[128,4096]{1,0:T(8,128)} fusion(s32[64]{0:T(128)S(1)} %fusion.136, f32[64,4096]{1,0:T(8,128)S(1)} %bitcast.237, f32[]{:T(128)} %constant.141.clone.1), kind=kCustom, calls=%fused_computation.150 | custom fusion | bytes 2097156 | tf_op jit(solution)/shard_map/scatter | solution.py:136
  162.9 5.1 %all-to-all-start.3 = ((f32[8,16,4096]{2,1,0:T(8,128)}), f32[8,16,4096]{2,1,0:T(8,128)S(1)}, u32[]{:S(2)}, u32[]{:S(2)}) async-start(f32[8,16,4096]{2,1,0:T(8,128)} %bitcast.15), calls=%async_computation.3 | async-start | bytes 4194304 | tf_op jit(solution)/shard_map/all_to_all | solution.py:139
  169.4 46.7 %all-to-all-done.3 = f32[8,16,4096]{2,1,0:T(8,128)S(1)} async-done(((f32[8,16,4096]{2,1,0:T(8,128)}), f32[8,16,4096]{2,1,0:T(8,128)S(1)}, u32[]{:S(2)}, u32[]{:S(2)}) %all-to-all-start.3) | async-done | bytes 2097184 | tf_op jit(solution)/shard_map/all_to_all | solution.py:139
  217.0 1.9 collective-permute-start
  218.9 2.4 %collective-permute-start.1 = (f32[1,8,4096]{2,1,0:T(8,128)S(1)}, f32[1,8,4096]{2,1,0:T(8,128)S(1)}, u32[]{:S(2)}, u32[]{:S(2)}) collective-permute-start(f32[1,8,4096]{2,1,0:T(8,128)S(1)} %get-tuple-element.139), channel_id=1, source_target_pairs={{1,0},{4,1},{5,4},{8,5},{9,8},{12,9},{13,12},{3,2},{6,3},{7,6},{10... | collective-permute-start | bytes 393224 | tf_op jit(solution)/shard_map/ppermute | solution.py:22
  221.3 3.9 %collective-permute-done.1 = f32[1,8,4096]{2,1,0:T(8,128)S(1)} collective-permute-done((f32[1,8,4096]{2,1,0:T(8,128)S(1)}, f32[1,8,4096]{2,1,0:T(8,128)S(1)}, u32[]{:S(2)}, u32[]{:S(2)}) %collective-permute-start.1) | collective-permute-done | bytes 131104 | tf_op jit(solution)/shard_map/ppermute | solution.py:22
  (156 shorter events, 77.5 us)
Async XLA Ops:
  0.0 13.7 %copy-start = (bf16[1,32,4096]{2,1,0:T(8,128)(2,1)S(1)}, bf16[1,32,4096]{2,1,0:T(8,128)(2,1)}, u32[]{:S(2)}) copy-start(bf16[1,32,4096]{2,1,0:T(8,128)(2,1)} %param.6) | copy-start | bytes 786436
  14.9 6.1 %copy-start.1 = (s32[1,64,1]{1,2,0:T(1,128)S(1)}, s32[1,64,1]{1,2,0:T(1,128)}, u32[]{:S(2)}) copy-start(s32[1,64,1]{1,2,0:T(1,128)} %param.8) | copy-start | bytes 772
  16.1 29.8 %all-to-all-start.2 = ((bf16[8,16,4096]{2,1,0:T(8,128)(2,1)}), bf16[8,16,4096]{2,1,0:T(8,128)(2,1)S(1)}, u32[]{:S(2)}, u32[]{:S(2)}) async-start(bf16[8,16,4096]{2,1,0:T(8,128)(2,1)} %broadcast_select_fusion), calls=%async_computation.2 | async-start | bytes 2097152 | tf_op jit(solution)/shard_map/all_to_all | solution.py:126
  45.9 117.0 %all-to-all-start = ((s32[8,16,1]{1,2,0:T(1,128)}), s32[8,16,1]{1,2,0:T(1,128)S(1)}, u32[]{:S(2)}, u32[]{:S(2)}) async-start(s32[8,16,1]{1,2,0:T(1,128)} %bitcast.5), calls=%async_computation | async-start | bytes 8192 | tf_op jit(solution)/shard_map/all_to_all | solution.py:140
  162.9 53.2 %all-to-all-start.3 = ((f32[8,16,4096]{2,1,0:T(8,128)}), f32[8,16,4096]{2,1,0:T(8,128)S(1)}, u32[]{:S(2)}, u32[]{:S(2)}) async-start(f32[8,16,4096]{2,1,0:T(8,128)} %bitcast.15), calls=%async_computation.3 | async-start | bytes 4194304 | tf_op jit(solution)/shard_map/all_to_all | solution.py:139
  217.0 4.3 %collective-permute-start = (f32[1,8,4096]{2,1,0:T(8,128)S(1)}, f32[1,8,4096]{2,1,0:T(8,128)S(1)}, u32[]{:S(2)}, u32[]{:S(2)}) collective-permute-start(f32[1,8,4096]{2,1,0:T(8,128)S(1)} %get-tuple-element.138), channel_id=1, source_target_pairs={{0,1},{1,4},{4,5},{5,8},{8,9},{9,12},{12,13},{2,3},{3,6},{6,7},{7,... | collective-permute-start | bytes 393224 | tf_op jit(solution)/shard_map/ppermute | solution.py:19
  218.9 6.3 %collective-permute-start.1 = (f32[1,8,4096]{2,1,0:T(8,128)S(1)}, f32[1,8,4096]{2,1,0:T(8,128)S(1)}, u32[]{:S(2)}, u32[]{:S(2)}) collective-permute-start(f32[1,8,4096]{2,1,0:T(8,128)S(1)} %get-tuple-element.139), channel_id=1, source_target_pairs={{1,0},{4,1},{5,4},{8,5},{9,8},{12,9},{13,12},{3,2},{6,3},{7,6},{10... | collective-permute-start | bytes 393224 | tf_op jit(solution)/shard_map/ppermute | solution.py:22
where the time goes:
time: 227 us; the launch traced here: 226 us
  matrix products  98 us (43%)
  waiting for transfers between devices  75.3 us (33%)
  starting transfers between devices  17.8 us (8%)
  local copies, waits for them, and re-layouts  14.4 us (6%)
  blocking collectives  11 us (5%)
  other arithmetic  8.43 us (4%)
    all_to_all x1, waiting for transfers between devices, on_device(): lax.all_to_all(score_buffer, ('tile', 'sub'), split_axis=0, concat_axis=0...  46.7 us
    all_to_all x1, waiting for transfers between devices, on_device(): lax.all_to_all(found, ('tile', 'sub'), split_axis=0, concat_axis=0, tiled...  24.7 us
    dot_general x8, matrix products, spectrum(): jnp.einsum('bkm,lm->bkl', first_real, sine_table, precision=precise)  15.5 us
    dot_general x8, matrix products, spectrum(): jnp.einsum('bkm,lm->bkl', first_real, cosine, precision=precise)  15.1 us
    dot_general x8, matrix products, spectrum(): jnp.einsum('bkm,lm->bkl', first_imag, sine_table, precision=precise)  15.1 us
    dot_general x8, matrix products, spectrum(): jnp.einsum('bkm,lm->bkl', first_imag, cosine, precision=precise)  15 us
    all_to_all x1, blocking collectives, on_device(): lax.all_to_all(requests, ('tile', 'sub'), split_axis=0, concat_axis=0, ti...  11 us
    dot_general x8, matrix products, spectrum(): first_real = jnp.einsum('kn,bnm->bkm', cosine, image, precision=precise)  6.31 us
  transfers between devices with their start and end apart: 5, of which 3 were waited for; matrix products, arithmetic and copies ran while one was open for 50% of the time, Pallas kernels for 0%

commit v1 on v0

--- a/solution.py
+++ b/solution.py
@@ -123,7 +123,18 @@
         ),
         axis=0,
     )
-    fetched = lax.all_to_all(found, ("tile", "sub"), split_axis=0, concat_axis=0, tiled=True)
+    ways, here = (lax.axis_size(("tile", "sub")), lax.axis_index(("tile", "sub")))
+    width_2 = found.shape[0] // ways
+    dims = list(found.shape)
+    dims[0] = width_2
+    height = dims[0]
+    dims[0] = height * ways
+    fetched = jnp.zeros(dims, found.dtype)
+    for mask in range(ways):
+        part = lax.dynamic_slice_in_dim(found, (here ^ mask) * width_2, width_2, axis=0)
+        if mask:
+            part = lax.ppermute(part, ("tile", "sub"), [(d, d ^ mask) for d in range(ways)])
+        fetched = lax.dynamic_update_slice_in_dim(fetched, part, (here ^ mask) * height, axis=0)
     own_chips = jnp.take(fetched.reshape(slot_amount, chip_side * chip_side), positions, axis=0)
 
     def match_own(chip_part, window_part):

time: 227 us -> 225 us (level)
  starting transfers between devices: 17.8 us -> 29.3 us
  blocking collectives: 11 us -> 0 us
  waiting for transfers between devices: 75.3 us -> 72.1 us
    all_to_all x1, waiting for transfers between devices: 24.7 us -> 3.3 us  [on_device(): lax.all_to_all(requests, ('tile', 'sub'), split_axis=0, concat_axis=0, ti...]
    ppermute x0 -> x7, waiting for transfers between devices: none -> 18.2 us  [on_device(): lax.ppermute(part, ('tile', 'sub'), [(d, d ^ mask) for d in range(ways)])]
    all_to_all x1 -> x0, blocking collectives: 11 us -> none  [on_device(): lax.all_to_all(requests, ('tile', 'sub'), split_axis=0, concat_axis=0, ti...]
    ppermute x0 -> x7, starting transfers between devices: none -> 10.9 us  [on_device(): lax.ppermute(part, ('tile', 'sub'), [(d, d ^ mask) for d in range(ways)])]
  transfers between devices with their start and end apart: 5 -> 12, of which waited for: 3 -> 5; matrix products, arithmetic and copies ran while one was open for 50% -> 52% of each run, Pallas kernels for 0% -> 0%
where the time goes in v1:
time: 225 us; the launch traced here: 224 us
  matrix products  98 us (44%)
  waiting for transfers between devices  72.1 us (32%)
  starting transfers between devices  29.3 us (13%)
  local copies, waits for them, and re-layouts  15.2 us (7%)
  other arithmetic  8.09 us (4%)
    all_to_all x1, waiting for transfers between devices, on_device(): lax.all_to_all(score_buffer, ('tile', 'sub'), split_axis=0, concat_axis=0...  46.7 us
    ppermute x7, waiting for transfers between devices, on_device(): lax.ppermute(part, ('tile', 'sub'), [(d, d ^ mask) for d in range(ways)])  18.2 us
    dot_general x8, matrix products, spectrum(): jnp.einsum('bkm,lm->bkl', first_real, sine_table, precision=precise)  15.5 us
    dot_general x8, matrix products, spectrum(): jnp.einsum('bkm,lm->bkl', first_real, cosine, precision=precise)  15.1 us
    dot_general x8, matrix products, spectrum(): jnp.einsum('bkm,lm->bkl', first_imag, sine_table, precision=precise)  15.1 us
    dot_general x8, matrix products, spectrum(): jnp.einsum('bkm,lm->bkl', first_imag, cosine, precision=precise)  15 us
    ppermute x7, starting transfers between devices, on_device(): lax.ppermute(part, ('tile', 'sub'), [(d, d ^ mask) for d in range(ways)])  10.9 us
    all_to_all x1, starting transfers between devices, on_device(): lax.all_to_all(requests, ('tile', 'sub'), split_axis=0, concat_axis=0, ti...  6.37 us
  transfers between devices with their start and end apart: 12, of which 5 were waited for; matrix products, arithmetic and copies ran while one was open for 52% of the time, Pallas kernels for 0%

profile of v1, /device:TPU:1, one launch (start us, length us, event | category | flops | bytes accessed | tf_op | source)
XLA Modules:
  0.0 224.3 jit_solution(10990145025154354654)
XLA Ops:
  3.2 6.4 %all-to-all-start.1 = ((s32[8,1,16]{2,1,0:T(1,128)}), s32[8,1,16]{2,1,0:T(1,128)S(1)}, u32[]{:S(2)}, u32[]{:S(2)}) async-start(s32[8,1,16]{2,1,0:T(1,128)} %bitcast.6), calls=%async_computation.1 | async-start | bytes 8192 | tf_op jit(solution)/shard_map/all_to_all | solution.py:122
  11.0 3.3 %all-to-all-done.1 = s32[8,1,16]{2,1,0:T(1,128)S(1)} async-done(((s32[8,1,16]{2,1,0:T(1,128)}), s32[8,1,16]{2,1,0:T(1,128)S(1)}, u32[]{:S(2)}, u32[]{:S(2)}) %all-to-all-start.1) | async-done | bytes 544 | tf_op jit(solution)/shard_map/all_to_all | solution.py:122
  14.3 3.9 %all-to-all-start = ((s32[8,16,1]{1,2,0:T(1,128)}), s32[8,16,1]{1,2,0:T(1,128)S(1)}, u32[]{:S(2)}, u32[]{:S(2)}) async-start(s32[8,16,1]{1,2,0:T(1,128)} %bitcast.5), calls=%async_computation | async-start | bytes 8192 | tf_op jit(solution)/shard_map/all_to_all | solution.py:151
  20.1 3.5 %collective-permute-start.6 = (bf16[1,16,4096]{2,1,0:T(8,128)(2,1)S(1)}, bf16[1,16,4096]{2,1,0:T(8,128)(2,1)S(1)}, u32[]{:S(2)}, u32[]{:S(2)}) collective-permute-start(bf16[1,16,4096]{2,1,0:T(8,128)(2,1)S(1)} %get-tuple-element.138), channel_id=1, source_target_pairs={{0,13},{1,12},{4,9},{5,8},{8,5},{9,4},{12,1},{13,0},{2,15},{3,14},... | collective-permute-start | bytes 393224 | tf_op jit(solution)/shard_map/ppermute | solution.py:136
  27.8 9.9 %collective-permute-done.1 = bf16[1,16,4096]{2,1,0:T(8,128)(2,1)S(1)} collective-permute-done((bf16[1,16,4096]{2,1,0:T(8,128)(2,1)S(1)}, bf16[1,16,4096]{2,1,0:T(8,128)(2,1)S(1)}, u32[]{:S(2)}, u32[]{:S(2)}) %collective-permute-start.1) | collective-permute-done | bytes 131104 | tf_op jit(solution)/shard_map/ppermute | solution.py:136
  37.7 3.1 %collective-permute-start.2 = (bf16[1,16,4096]{2,1,0:T(8,128)(2,1)S(1)}, bf16[1,16,4096]{2,1,0:T(8,128)(2,1)S(1)}, u32[]{:S(2)}, u32[]{:S(2)}) collective-permute-start(bf16[1,16,4096]{2,1,0:T(8,128)(2,1)S(1)} %get-tuple-element.142), channel_id=1, source_target_pairs={{0,5},{1,4},{4,1},{5,0},{8,13},{9,12},{12,9},{13,8},{2,7},{3,6},{6... | collective-permute-start | bytes 393224 | tf_op jit(solution)/shard_map/ppermute | solution.py:136
  40.7 8.3 %collective-permute-done.2 = bf16[1,16,4096]{2,1,0:T(8,128)(2,1)S(1)} collective-permute-done((bf16[1,16,4096]{2,1,0:T(8,128)(2,1)S(1)}, bf16[1,16,4096]{2,1,0:T(8,128)(2,1)S(1)}, u32[]{:S(2)}, u32[]{:S(2)}) %collective-permute-start.2) | collective-permute-done | bytes 131104 | tf_op jit(solution)/shard_map/ppermute | solution.py:136
  50.2 109.4 %while.14 = (s32[]{:T(128)}, f32[4,16,4096]{2,1,0:T(8,128)S(1)}, bf16[4,16,4096]{2,1,0:T(8,128)(2,1)S(1)}, bf16[4,16,16384]{2,1,0:T(8,128)(2,1)}, s32[]{:T(128)}) while((s32[]{:T(128)}, f32[4,16,4096]{2,1,0:T(8,128)S(1)}, bf16[4,16,4096]{2,1,0:T(8,128)(2,1)S(1)}, bf16[4,16,16384]{2,1,0:T(8,128)(2,1)}, s32[]{:T(128)}) %tuple.46), condition=%wide.region_5.6_spmd.clone.clone, body=%wide.region_2.5_spmd.clone.clone.sunk | while | flops 4872994816 | bytes 46598104 | solution.py:94
  57.4 2.0 fusion.248
  59.4 1.9 convolution_add_fusion.5
  61.4 1.9 fusion.252
  63.3 1.9 convolution_subtract_fusion.5
  70.8 1.9 multiply_subtract_fusion.2
  84.7 2.0 fusion.248
  86.7 1.9 convolution_add_fusion.5
  88.6 1.9 fusion.252
  90.6 1.9 convolution_subtract_fusion.5
  112.0 2.0 fusion.248
  113.9 1.9 convolution_add_fusion.5
  115.9 1.9 fusion.252
  117.8 1.9 convolution_subtract_fusion.5
  125.3 1.9 multiply_subtract_fusion.2
  139.2 2.0 fusion.248
  141.2 1.9 convolution_add_fusion.5
  143.1 1.9 fusion.252
  145.1 1.9 convolution_subtract_fusion.5
  152.5 1.9 multiply_subtract_fusion.2
  159.6 2.6 %scatter_custom_fusion.1 = f32[128,4096]{1,0:T(8,128)} fusion(s32[64]{0:T(128)S(1)} %fusion.136, f32[64,4096]{1,0:T(8,128)S(1)} %bitcast.236, f32[]{:T(128)} %constant.156.clone.1), kind=kCustom, calls=%fused_computation.150 | custom fusion | bytes 2097156 | tf_op jit(solution)/shard_map/scatter | solution.py:147
  162.2 3.9 %all-to-all-start.2 = ((f32[8,16,4096]{2,1,0:T(8,128)}), f32[8,16,4096]{2,1,0:T(8,128)S(1)}, u32[]{:S(2)}, u32[]{:S(2)}) async-start(f32[8,16,4096]{2,1,0:T(8,128)} %bitcast.15), calls=%async_computation.2 | async-start | bytes 4194304 | tf_op jit(solution)/shard_map/all_to_all | solution.py:150
  167.5 46.7 %all-to-all-done.2 = f32[8,16,4096]{2,1,0:T(8,128)S(1)} async-done(((f32[8,16,4096]{2,1,0:T(8,128)}), f32[8,16,4096]{2,1,0:T(8,128)S(1)}, u32[]{:S(2)}, u32[]{:S(2)}) %all-to-all-start.2) | async-done | bytes 2097184 | tf_op jit(solution)/shard_map/all_to_all | solution.py:150
  217.0 2.4 %collective-permute-start.8 = (f32[1,8,4096]{2,1,0:T(8,128)S(1)}, f32[1,8,4096]{2,1,0:T(8,128)S(1)}, u32[]{:S(2)}, u32[]{:S(2)}) collective-permute-start(f32[1,8,4096]{2,1,0:T(8,128)S(1)} %get-tuple-element.147), channel_id=1, source_target_pairs={{1,0},{4,1},{5,4},{8,5},{9,8},{12,9},{13,12},{3,2},{6,3},{7,6},{10... | collective-permute-start | bytes 393224 | tf_op jit(solution)/shard_map/ppermute | solution.py:22
  219.5 3.9 %collective-permute-done.8 = f32[1,8,4096]{2,1,0:T(8,128)S(1)} collective-permute-done((f32[1,8,4096]{2,1,0:T(8,128)S(1)}, f32[1,8,4096]{2,1,0:T(8,128)S(1)}, u32[]{:S(2)}, u32[]{:S(2)}) %collective-permute-start.8) | collective-permute-done | bytes 131104 | tf_op jit(solution)/shard_map/ppermute | solution.py:22
  (176 shorter events, 88.0 us)
Async XLA Ops:
  0.0 18.3 %copy-start = (bf16[1,32,4096]{2,1,0:T(8,128)(2,1)S(1)}, bf16[1,32,4096]{2,1,0:T(8,128)(2,1)}, u32[]{:S(2)}) copy-start(bf16[1,32,4096]{2,1,0:T(8,128)(2,1)} %param.6) | copy-start | bytes 786436
  3.2 11.2 %all-to-all-start.1 = ((s32[8,1,16]{2,1,0:T(1,128)}), s32[8,1,16]{2,1,0:T(1,128)S(1)}, u32[]{:S(2)}, u32[]{:S(2)}) async-start(s32[8,1,16]{2,1,0:T(1,128)} %bitcast.6), calls=%async_computation.1 | async-start | bytes 8192 | tf_op jit(solution)/shard_map/all_to_all | solution.py:122
  14.3 147.9 %all-to-all-start = ((s32[8,16,1]{1,2,0:T(1,128)}), s32[8,16,1]{1,2,0:T(1,128)S(1)}, u32[]{:S(2)}, u32[]{:S(2)}) async-start(s32[8,16,1]{1,2,0:T(1,128)} %bitcast.5), calls=%async_computation | async-start | bytes 8192 | tf_op jit(solution)/shard_map/all_to_all | solution.py:151
  19.9 6.5 %collective-permute-start = (bf16[1,16,4096]{2,1,0:T(8,128)(2,1)S(1)}, bf16[1,16,4096]{2,1,0:T(8,128)(2,1)S(1)}, u32[]{:S(2)}, u32[]{:S(2)}) collective-permute-start(bf16[1,16,4096]{2,1,0:T(8,128)(2,1)S(1)} %get-tuple-element.144), channel_id=1, source_target_pairs={{0,1},{1,0},{4,5},{5,4},{8,9},{9,8},{12,13},{13,12},{2,3},{3,2},{6... | collective-permute-start | bytes 393224 | tf_op jit(solution)/shard_map/ppermute | solution.py:136
  20.1 29.0 %collective-permute-start.6 = (bf16[1,16,4096]{2,1,0:T(8,128)(2,1)S(1)}, bf16[1,16,4096]{2,1,0:T(8,128)(2,1)S(1)}, u32[]{:S(2)}, u32[]{:S(2)}) collective-permute-start(bf16[1,16,4096]{2,1,0:T(8,128)(2,1)S(1)} %get-tuple-element.138), channel_id=1, source_target_pairs={{0,13},{1,12},{4,9},{5,8},{8,5},{9,4},{12,1},{13,0},{2,15},{3,14},... | collective-permute-start | bytes 393224 | tf_op jit(solution)/shard_map/ppermute | solution.py:136
  23.6 25.5 %collective-permute-start.5 = (bf16[1,16,4096]{2,1,0:T(8,128)(2,1)S(1)}, bf16[1,16,4096]{2,1,0:T(8,128)(2,1)S(1)}, u32[]{:S(2)}, u32[]{:S(2)}) collective-permute-start(bf16[1,16,4096]{2,1,0:T(8,128)(2,1)S(1)} %get-tuple-element.139), channel_id=1, source_target_pairs={{0,12},{1,13},{4,8},{5,9},{8,4},{9,5},{12,0},{13,1},{2,14},{3,15},... | collective-permute-start | bytes 393224 | tf_op jit(solution)/shard_map/ppermute | solution.py:136
  23.7 25.3 %collective-permute-start.4 = (bf16[1,16,4096]{2,1,0:T(8,128)(2,1)S(1)}, bf16[1,16,4096]{2,1,0:T(8,128)(2,1)S(1)}, u32[]{:S(2)}, u32[]{:S(2)}) collective-permute-start(bf16[1,16,4096]{2,1,0:T(8,128)(2,1)S(1)} %get-tuple-element.140), channel_id=1, source_target_pairs={{0,9},{1,8},{4,13},{5,12},{8,1},{9,0},{12,5},{13,4},{2,11},{3,10},... | collective-permute-start | bytes 393224 | tf_op jit(solution)/shard_map/ppermute | solution.py:136
  24.8 24.3 %collective-permute-start.3 = (bf16[1,16,4096]{2,1,0:T(8,128)(2,1)S(1)}, bf16[1,16,4096]{2,1,0:T(8,128)(2,1)S(1)}, u32[]{:S(2)}, u32[]{:S(2)}) collective-permute-start(bf16[1,16,4096]{2,1,0:T(8,128)(2,1)S(1)} %get-tuple-element.141), channel_id=1, source_target_pairs={{0,8},{1,9},{4,12},{5,13},{8,0},{9,1},{12,4},{13,5},{2,10},{3,11},... | collective-permute-start | bytes 393224 | tf_op jit(solution)/shard_map/ppermute | solution.py:136
  26.4 11.3 %collective-permute-start.1 = (bf16[1,16,4096]{2,1,0:T(8,128)(2,1)S(1)}, bf16[1,16,4096]{2,1,0:T(8,128)(2,1)S(1)}, u32[]{:S(2)}, u32[]{:S(2)}) collective-permute-start(bf16[1,16,4096]{2,1,0:T(8,128)(2,1)S(1)} %get-tuple-element.143), channel_id=1, source_target_pairs={{0,4},{1,5},{4,0},{5,1},{8,12},{9,13},{12,8},{13,9},{2,6},{3,7},{6... | collective-permute-start | bytes 393224 | tf_op jit(solution)/shard_map/ppermute | solution.py:136
  37.7 11.3 %collective-permute-start.2 = (bf16[1,16,4096]{2,1,0:T(8,128)(2,1)S(1)}, bf16[1,16,4096]{2,1,0:T(8,128)(2,1)S(1)}, u32[]{:S(2)}, u32[]{:S(2)}) collective-permute-start(bf16[1,16,4096]{2,1,0:T(8,128)(2,1)S(1)} %get-tuple-element.142), channel_id=1, source_target_pairs={{0,5},{1,4},{4,1},{5,0},{8,13},{9,12},{12,9},{13,8},{2,7},{3,6},{6... | collective-permute-start | bytes 393224 | tf_op jit(solution)/shard_map/ppermute | solution.py:136
  162.2 52.0 %all-to-all-start.2 = ((f32[8,16,4096]{2,1,0:T(8,128)}), f32[8,16,4096]{2,1,0:T(8,128)S(1)}, u32[]{:S(2)}, u32[]{:S(2)}) async-start(f32[8,16,4096]{2,1,0:T(8,128)} %bitcast.15), calls=%async_computation.2 | async-start | bytes 4194304 | tf_op jit(solution)/shard_map/all_to_all | solution.py:150
  215.1 4.3 %collective-permute-start.7 = (f32[1,8,4096]{2,1,0:T(8,128)S(1)}, f32[1,8,4096]{2,1,0:T(8,128)S(1)}, u32[]{:S(2)}, u32[]{:S(2)}) collective-permute-start(f32[1,8,4096]{2,1,0:T(8,128)S(1)} %get-tuple-element.146), channel_id=1, source_target_pairs={{0,1},{1,4},{4,5},{5,8},{8,9},{9,12},{12,13},{2,3},{3,6},{6,7},{7,... | collective-permute-start | bytes 393224 | tf_op jit(solution)/shard_map/ppermute | solution.py:19
  217.0 6.3 %collective-permute-start.8 = (f32[1,8,4096]{2,1,0:T(8,128)S(1)}, f32[1,8,4096]{2,1,0:T(8,128)S(1)}, u32[]{:S(2)}, u32[]{:S(2)}) collective-permute-start(f32[1,8,4096]{2,1,0:T(8,128)S(1)} %get-tuple-element.147), channel_id=1, source_target_pairs={{1,0},{4,1},{5,4},{8,5},{9,8},{12,9},{13,12},{3,2},{6,3},{7,6},{10... | collective-permute-start | bytes 393224 | tf_op jit(solution)/shard_map/ppermute | solution.py:22
